TPU v7x, 32 devices: a whole 2x2x4 slice. The times are simulated.
32 devices in a mesh: grp: 2 (over y), frame: 4 (over x, core), band: 4 (over z).
Axes of the slice: x: 2, y: 2, z: 4, core: 2. Of those that a mesh axis runs over, the one named last changes fastest.
Arguments:
- features: bfloat16 [16, 64, 128, 256], P(('grp', 'frame'), 'band'), parts along dimension 0, may hold values from -6 to 6
- space_kernel: bfloat16 [3, 3, 256, 256], replicated, may hold values from -0.125 to 0.125
- space_gain: float32 [256], replicated, may hold values from 0.5 to 2
- space_bias: float32 [256], replicated, may hold values from -3 to 3
- time_kernel: bfloat16 [3, 256, 256], replicated, may hold values from -0.21875 to 0.21875
- time_gain: float32 [256], replicated, may hold values from 0.5 to 2
- time_bias: float32 [256], replicated, may hold values from -3 to 3
Outputs:
- decoded: bfloat16 [16, 64, 128, 256], P(('grp', 'frame'), 'band'), parts along dimension 0
There are 2 independent parts, one for each index of `grp`. A program takes and returns all parts, laid end to end along the dimension named above; an argument that names none is the same for every part. Nothing has to cross between parts.
All inputs are finite; a program needn't handle non-finite values.
Results may differ from a plain program's by a relative error of at most 0.0056.
Values may be sent and summed in bfloat16 or wider, within the bound.
A program may use at most 64 MiB of HBM per device.

v0:
```python
import jax
import jax.numpy as jnp
from jax import lax
from jax.sharding import PartitionSpec as P


def with_halo(array, sides, width):
    for axis, dim in sides:
        count, length = (lax.axis_size(axis), array.shape[dim])
        up = [(i, (i + 1) % count) for i in range(count - 1)]
        down = [(j, i) for i, j in up]
        last = lax.slice_in_dim(array, length - width, length, axis=dim)
        first = lax.slice_in_dim(array, 0, width, axis=dim)
        before = lax.ppermute(last, axis, up)
        after = lax.ppermute(first, axis, down)
        array = jnp.concatenate([before, array, after], axis=dim)
    return array


def passed_along(array, axis, by):
    count = lax.axis_size(axis)
    pairs = [(i, i + by) for i in range(count) if 0 <= i + by < count]
    return lax.ppermute(array, axis, pairs)


def rms_silu(values, gain_vector):
    widened = values.astype(jnp.float32)
    scaled = (
        widened
        * lax.rsqrt(jnp.mean(widened * widened, axis=-1, keepdims=True) + 1e-06)
        * gain_vector
    )
    return jax.nn.silu(scaled).astype(jnp.bfloat16)


def lag_product(frames_in, kernel_slice):
    channels = frames_in.shape[-1]
    product = jnp.dot(
        frames_in.reshape(-1, channels), kernel_slice, preferred_element_type=jnp.float32
    )
    return product.reshape(frames_in.shape[:-1] + (kernel_slice.shape[1],))


def body(features, space_kernel, space_gain, space_bias, time_kernel, time_gain, time_bias):
    frame_count, rows_count, cols_count, channels = features.shape
    normed = rms_silu(features, space_gain)
    padded = with_halo(normed, (("band", 1),), 1)
    padded = jnp.pad(padded, ((0, 0), (0, 0), (1, 1), (0, 0)))
    summed = None
    for tap_row in range(3):
        for tap_col in range(3):
            window = padded[
                :, tap_row : tap_row + rows_count, tap_col : tap_col + cols_count
            ].reshape(-1, channels)
            product = jnp.dot(
                window, space_kernel[tap_row, tap_col], preferred_element_type=jnp.float32
            )
            summed = product if summed is None else summed + product
    spatial = summed.reshape(features.shape)
    hidden = (features.astype(jnp.float32) + spatial + space_bias).astype(jnp.bfloat16)
    hidden = lax.optimization_barrier(hidden)
    normed_time = rms_silu(hidden, time_gain)
    local_sum = lag_product(normed_time, time_kernel[0])
    for time_lag in range(1, 3):
        shifted = lag_product(normed_time[: frame_count - time_lag], time_kernel[time_lag])
        local_sum = local_sum + jnp.pad(shifted, ((time_lag, 0), (0, 0), (0, 0), (0, 0)))
    earlier = passed_along(normed_time, "frame", 1)
    for time_lag in range(1, 3):
        remote = lag_product(earlier[2 - time_lag :], time_kernel[time_lag])
        local_sum = local_sum + jnp.pad(
            remote, ((0, frame_count - time_lag), (0, 0), (0, 0), (0, 0))
        )
    temporal = local_sum.astype(jnp.bfloat16)
    temporal = lax.optimization_barrier(temporal)
    decoded = hidden.astype(jnp.float32) + temporal.astype(jnp.float32) + time_bias
    return decoded.astype(jnp.bfloat16)


def solution(mesh):
    return jax.shard_map(
        body,
        mesh=mesh,
        in_specs=(P(("grp", "frame"), "band", None, None), P(), P(), P(), P(), P(), P()),
        out_specs=P(("grp", "frame"), "band", None, None),
        check_vma=False,
    )
```

profile of v0, /device:TPU:14, one launch (start us, length us, event | category | flops | bytes accessed | tf_op | source)
XLA Modules:
  0.0 61.6 jit_solution(18141599922598498462)
XLA Ops:
  0.0 0.0 copy-start
  0.0 0.0 copy-start.3
  0.0 2.4 %fusion.2 = f32[2,16,128]{2,1,0:T(8,128)S(1)} fusion(bf16[2,16,128,256]{3,2,1,0:T(8,128)(2,1)} %param.7), kind=kLoop, calls=%fused_computation.17 | loop fusion | flops 3141632 | bytes 2113536 | tf_op jit(solution)/shard_map/reduce_sum | solution.py:30
  2.4 0.0 copy-done
  2.4 0.0 copy-done.3
  2.4 1.4 %fusion.9 = bf16[2,16,128,256]{3,2,1,0:T(8,128)(2,1)S(1)} fusion(bf16[2,16,128,256]{3,2,1,0:T(8,128)(2,1)S(1)} %copy-done, f32[256]{0:T(256)S(1)} %copy-done.3, f32[2,16,128]{2,1,0:T(8,128)S(1)} %add_rsqrt_fusion.1), kind=kLoop, calls=%fused_computation.24 | loop fusion | flops 8388608 | bytes 4211712 | tf_op jit(solution)/shard_map/convert_element_type | solution.py:33
  3.8 3.5 %collective-permute-start = (bf16[2,1,128,256]{3,2,1,0:T(8,128)(2,1)S(1)}, bf16[2,1,128,256]{3,2,1,0:T(8,128)(2,1)S(1)}, u32[]{:S(2)}, u32[]{:S(2)}) collective-permute-start(bf16[2,1,128,256]{3,2,1,0:T(8,128)(2,1)S(1)} %get-tuple-element.13), channel_id=1, source_target_pairs={{0,1},{1,2},{2,3},{4,5},{5,6},{6,7},{8,9},{9,10},{10,11},{12,13},{... | collective-permute-start | bytes 393224 | tf_op jit(solution)/shard_map/ppermute | solution.py:14
  7.3 2.4 %collective-permute-start.1 = (bf16[2,1,128,256]{3,2,1,0:T(8,128)(2,1)S(1)}, bf16[2,1,128,256]{3,2,1,0:T(8,128)(2,1)S(1)}, u32[]{:S(2)}, u32[]{:S(2)}) collective-permute-start(bf16[2,1,128,256]{3,2,1,0:T(8,128)(2,1)S(1)} %get-tuple-element.14), channel_id=1, source_target_pairs={{1,0},{2,1},{3,2},{5,4},{6,5},{7,6},{9,8},{10,9},{11,10},{13,12},{... | collective-permute-start | bytes 393224 | tf_op jit(solution)/shard_map/ppermute | solution.py:15
  9.7 1.3 %collective-permute-done = bf16[2,1,128,256]{3,2,1,0:T(8,128)(2,1)S(1)} collective-permute-done((bf16[2,1,128,256]{3,2,1,0:T(8,128)(2,1)S(1)}, bf16[2,1,128,256]{3,2,1,0:T(8,128)(2,1)S(1)}, u32[]{:S(2)}, u32[]{:S(2)}) %collective-permute-start) | collective-permute-done | bytes 131104 | tf_op jit(solution)/shard_map/ppermute | solution.py:14
  11.0 3.2 %collective-permute-done.1 = bf16[2,1,128,256]{3,2,1,0:T(8,128)(2,1)S(1)} collective-permute-done((bf16[2,1,128,256]{3,2,1,0:T(8,128)(2,1)S(1)}, bf16[2,1,128,256]{3,2,1,0:T(8,128)(2,1)S(1)}, u32[]{:S(2)}, u32[]{:S(2)}) %collective-permute-start.1) | collective-permute-done | bytes 131104 | tf_op jit(solution)/shard_map/ppermute | solution.py:15
  14.2 1.1 %fusion.26 = bf16[2,18,130,256]{3,2,1,0:T(8,128)(2,1)S(1)} fusion(bf16[2,1,128,256]{3,2,1,0:T(8,128)(2,1)S(1)} %collective-permute-done.1, bf16[2,16,128,256]{3,2,1,0:T(8,128)(2,1)S(1)} %fusion.9, bf16[2,1,128,256]{3,2,1,0:T(8,128)(2,1)S(1)} %collective-permute-done), kind=kLoop, calls=%fused_computation.42 | loop fusion | flops 14376960 | bytes 4755456 | tf_op jit(solution)/shard_map/concatenate | solution.py:16
  15.3 0.0 copy-start.1
  15.3 5.2 %fusion.56 = (bf16[2,16,128,256]{3,2,1,0:T(8,128)(2,1)S(1)}, bf16[2,16,128,256]{3,2,1,0:T(8,128)(2,1)S(1)}, bf16[2,16,128,256]{3,2,1,0:T(8,128)(2,1)S(1)}, bf16[...) fusion(bf16[2,18,130,256]{3,2,1,0:T(8,128)(2,1)S(1)} %fusion.26), kind=kLoop, calls=%fused_computation.80 | loop fusion | bytes 25165824 | tf_op jit(solution)/shard_map/slice | solution.py:52
  20.5 0.0 copy-done.1
  20.5 0.7 %fusion.41 = f32[4096,256]{1,0:T(8,128)S(1)} fusion(bf16[4096,256]{1,0:T(8,128)(2,1)S(1)} %bitcast.81, bf16[3,3,256,256]{3,2,1,0:T(8,128)(2,1)S(1)} %copy-done.1), kind=kOutput, calls=%fused_computation.63 | convolution fusion | flops 536870912 | bytes 6422528 | tf_op jit(solution)/shard_map/dot_general | solution.py:55
  21.2 0.7 %fusion.32 = f32[4096,256]{1,0:T(8,128)S(1)} fusion(bf16[4096,256]{1,0:T(8,128)(2,1)S(1)} %bitcast.80, bf16[3,3,256,256]{3,2,1,0:T(8,128)(2,1)S(1)} %copy-done.1), kind=kOutput, calls=%fused_computation.54 | convolution fusion | flops 536870912 | bytes 6422528 | tf_op jit(solution)/shard_map/dot_general | solution.py:55
  21.9 0.3 pad_maximum_fusion
  22.2 0.8 %convolution_add_fusion.6 = f32[4096,256]{1,0:T(8,128)S(1)} fusion(f32[4096,256]{1,0:T(8,128)S(1)} %fusion.41, bf16[4096,256]{1,0:T(8,128)(2,1)S(1)} %bitcast.87, bf16[3,3,256,256]{3,2,1,0:T(8,128)(2,1)S(1)} %copy-done.1), kind=kOutput, calls=%fused_computation.15 | convolution fusion | flops 537919488 | bytes 10616832 | tf_op jit(solution)/shard_map/dot_general | solution.py:55
  23.0 0.8 %convolution_add_fusion.5 = f32[4096,256]{1,0:T(8,128)S(1)} fusion(f32[4096,256]{1,0:T(8,128)S(1)} %convolution_add_fusion.6, bf16[4096,256]{1,0:T(8,128)(2,1)S(1)} %bitcast.86, bf16[3,3,256,256]{3,2,1,0:T(8,128)(2,1)S(1)} %copy-done.1), kind=kOutput, calls=%fused_computation.14 | convolution fusion | flops 537919488 | bytes 10616832 | tf_op jit(solution)/shard_map/dot_general | solution.py:55
  23.7 0.8 %convolution_add_fusion.4 = f32[4096,256]{1,0:T(8,128)S(1)} fusion(f32[4096,256]{1,0:T(8,128)S(1)} %convolution_add_fusion.5, bf16[4096,256]{1,0:T(8,128)(2,1)S(1)} %bitcast.85, bf16[3,3,256,256]{3,2,1,0:T(8,128)(2,1)S(1)} %copy-done.1), kind=kOutput, calls=%fused_computation.13 | convolution fusion | flops 537919488 | bytes 10616832 | tf_op jit(solution)/shard_map/dot_general | solution.py:55
  24.5 0.8 %convolution_add_fusion.3 = f32[4096,256]{1,0:T(8,128)S(1)} fusion(f32[4096,256]{1,0:T(8,128)S(1)} %convolution_add_fusion.4, bf16[4096,256]{1,0:T(8,128)(2,1)S(1)} %bitcast.78, bf16[3,3,256,256]{3,2,1,0:T(8,128)(2,1)S(1)} %copy-done.1), kind=kOutput, calls=%fused_computation.12 | convolution fusion | flops 537919488 | bytes 10616832 | tf_op jit(solution)/shard_map/dot_general | solution.py:55
  25.3 0.8 %convolution_add_fusion.2 = f32[4096,256]{1,0:T(8,128)S(1)} fusion(f32[4096,256]{1,0:T(8,128)S(1)} %convolution_add_fusion.3, bf16[4096,256]{1,0:T(8,128)(2,1)S(1)} %bitcast.84, bf16[3,3,256,256]{3,2,1,0:T(8,128)(2,1)S(1)} %copy-done.1), kind=kOutput, calls=%fused_computation.11 | convolution fusion | flops 537919488 | bytes 10616832 | tf_op jit(solution)/shard_map/dot_general | solution.py:55
  26.1 0.8 %convolution_add_fusion.1 = f32[4096,256]{1,0:T(8,128)S(1)} fusion(f32[4096,256]{1,0:T(8,128)S(1)} %convolution_add_fusion.2, bf16[4096,256]{1,0:T(8,128)(2,1)S(1)} %bitcast.83, bf16[3,3,256,256]{3,2,1,0:T(8,128)(2,1)S(1)} %copy-done.1), kind=kOutput, calls=%fused_computation.10 | convolution fusion | flops 537919488 | bytes 10616832 | tf_op jit(solution)/shard_map/dot_general | solution.py:55
  26.9 0.0 copy-start.4
  26.9 0.9 %fusion = f32[4096,256]{1,0:T(8,128)S(1)} fusion(f32[4096,256]{1,0:T(8,128)S(1)} %fusion.32, f32[4096,256]{1,0:T(8,128)S(1)} %convolution_add_fusion.1, bf16[4096,256]{1,0:T(8,128)(2,1)S(1)} %bitcast.82, bf16[3,3,256,256]{3,2,1,0:T(8,128)(2,1)S(1)} %copy-done.1), kind=kOutput, calls=%fused_computation.9 | convolution fusion | flops 538968064 | bytes 14811136 | tf_op jit(solution)/shard_map/dot_general | solution.py:55
  27.8 0.0 copy-done.4
  27.8 0.8 %fusion.11 = bf16[2,16,128,256]{3,2,1,0:T(8,128)(2,1)S(1)} fusion(f32[2,16,128,256]{3,2,1,0:T(8,128)S(1)} %bitcast.79, bf16[2,16,128,256]{3,2,1,0:T(8,128)(2,1)S(1)} %copy-done, f32[256]{0:T(256)S(1)} %copy-done.4), kind=kLoop, calls=%fused_computation.26 | loop fusion | flops 4194304 | bytes 8389632 | tf_op jit(solution)/shard_map/convert_element_type | solution.py:60
  28.7 0.0 copy-start.5
  28.7 0.6 fusion.12
  29.3 0.0 copy-done.5
  29.4 0.0 copy-start.2
  29.4 1.4 %fusion.19 = bf16[2,16,128,256]{3,2,1,0:T(8,128)(2,1)S(1)} fusion(bf16[2,16,128,256]{3,2,1,0:T(8,128)(2,1)S(1)} %fusion.11, f32[256]{0:T(256)S(1)} %copy-done.5, f32[2,16,128]{2,1,0:T(8,128)S(1)} %add_rsqrt_fusion), kind=kLoop, calls=%fused_computation.34 | loop fusion | flops 8388608 | bytes 4211712 | tf_op jit(solution)/shard_map/convert_element_type | solution.py:33
  30.7 2.1 %collective-permute-start.2 = (bf16[2,16,128,256]{3,2,1,0:T(8,128)(2,1)S(1)}, bf16[2,16,128,256]{3,2,1,0:T(8,128)(2,1)S(1)}, u32[]{:S(2)}, u32[]{:S(2)}) collective-permute-start(bf16[2,16,128,256]{3,2,1,0:T(8,128)(2,1)S(1)} %fusion.19), channel_id=1, source_target_pairs={{0,4},{4,8},{8,12},{1,5},{5,9},{9,13},{2,6},{6,10},{10,14},{3,7},{... | collective-permute-start | bytes 6291464 | tf_op jit(solution)/shard_map/ppermute | solution.py:23
  32.9 0.0 copy-done.2
  32.9 0.4 convolution_bitcast_fusion.1
  33.3 0.7 %fusion.28 = f32[2,16,128,256]{3,2,1,0:T(8,128)S(1)} fusion(bf16[2,16,128,256]{3,2,1,0:T(8,128)(2,1)S(1)} %fusion.19, bf16[3,256,256]{2,1,0:T(8,128)(2,1)S(1)} %copy-done.2), kind=kOutput, calls=%fused_computation.50 | convolution fusion | flops 536870912 | bytes 6422528 | tf_op jit(solution)/shard_map/dot_general | solution.py:38
  34.0 24.1 %collective-permute-done.2 = bf16[2,16,128,256]{3,2,1,0:T(8,128)(2,1)S(1)} collective-permute-done((bf16[2,16,128,256]{3,2,1,0:T(8,128)(2,1)S(1)}, bf16[2,16,128,256]{3,2,1,0:T(8,128)(2,1)S(1)}, u32[]{:S(2)}, u32[]{:S(2)}) %collective-permute-start.2) | collective-permute-done | bytes 2097184 | tf_op jit(solution)/shard_map/ppermute | solution.py:23
  58.1 0.4 convolution_bitcast_fusion
  58.5 0.0 copy-start.6
  58.5 0.9 %add_convert_fusion = bf16[2,16,128,256]{3,2,1,0:T(8,128)(2,1)S(1)} fusion(f32[1,16,128,256]{3,2,1,0:T(8,128)S(1)} %convolution_bitcast_fusion, f32[2,16,128,256]{3,2,1,0:T(8,128)S(1)} %fusion.28, f32[1,16,128,256]{3,2,1,0:T(8,128)S(1)} %convolution_bitcast_fusion.1, bf16[2,16,128,256]{3,2,1,0:T(8,128)(2,1)S(1)} %collective-permute-done.2, ...), kind=kOutput, calls=%fused_computation.37 | convolution fusion | flops 541065216 | bytes 12713984 | tf_op jit(solution)/shard_map/dot_general | solution.py:38
  59.4 0.0 copy-done.6
  59.4 2.2 %fusion.21 = bf16[2,16,128,256]{3,2,1,0:T(8,128)(2,1)} fusion(bf16[2,16,128,256]{3,2,1,0:T(8,128)(2,1)S(1)} %fusion.11, bf16[2,16,128,256]{3,2,1,0:T(8,128)(2,1)S(1)} %add_convert_fusion, f32[256]{0:T(256)S(1)} %copy-done.6), kind=kLoop, calls=%fused_computation.36 | loop fusion | flops 5242880 | bytes 6292480 | tf_op jit(solution)/shard_map/convert_element_type | solution.py:76
  (3 shorter events, 0.0 us)
Async XLA Ops:
  0.0 2.4 %copy-start = (bf16[2,16,128,256]{3,2,1,0:T(8,128)(2,1)S(1)}, bf16[2,16,128,256]{3,2,1,0:T(8,128)(2,1)}, u32[]{:S(2)}) copy-start(bf16[2,16,128,256]{3,2,1,0:T(8,128)(2,1)} %param.7) | copy-start | bytes 6291460
  0.0 2.4 %copy-start.3 = (f32[256]{0:T(256)S(1)}, f32[256]{0:T(256)}, u32[]{:S(2)}) copy-start(f32[256]{0:T(256)} %param.9) | copy-start | bytes 3076
  3.8 7.1 %collective-permute-start = (bf16[2,1,128,256]{3,2,1,0:T(8,128)(2,1)S(1)}, bf16[2,1,128,256]{3,2,1,0:T(8,128)(2,1)S(1)}, u32[]{:S(2)}, u32[]{:S(2)}) collective-permute-start(bf16[2,1,128,256]{3,2,1,0:T(8,128)(2,1)S(1)} %get-tuple-element.13), channel_id=1, source_target_pairs={{0,1},{1,2},{2,3},{4,5},{5,6},{6,7},{8,9},{9,10},{10,11},{12,13},{... | collective-permute-start | bytes 393224 | tf_op jit(solution)/shard_map/ppermute | solution.py:14
  7.3 6.9 %collective-permute-start.1 = (bf16[2,1,128,256]{3,2,1,0:T(8,128)(2,1)S(1)}, bf16[2,1,128,256]{3,2,1,0:T(8,128)(2,1)S(1)}, u32[]{:S(2)}, u32[]{:S(2)}) collective-permute-start(bf16[2,1,128,256]{3,2,1,0:T(8,128)(2,1)S(1)} %get-tuple-element.14), channel_id=1, source_target_pairs={{1,0},{2,1},{3,2},{5,4},{6,5},{7,6},{9,8},{10,9},{11,10},{13,12},{... | collective-permute-start | bytes 393224 | tf_op jit(solution)/shard_map/ppermute | solution.py:15
  15.3 5.2 %copy-start.1 = (bf16[3,3,256,256]{3,2,1,0:T(8,128)(2,1)S(1)}, bf16[3,3,256,256]{3,2,1,0:T(8,128)(2,1)}, u32[]{:S(2)}) copy-start(bf16[3,3,256,256]{3,2,1,0:T(8,128)(2,1)} %param.8) | copy-start | bytes 3538948
  26.9 1.0 %copy-start.4 = (f32[256]{0:T(256)S(1)}, f32[256]{0:T(256)}, u32[]{:S(2)}) copy-start(f32[256]{0:T(256)} %param.10) | copy-start | bytes 3076
  28.7 0.7 %copy-start.5 = (f32[256]{0:T(256)S(1)}, f32[256]{0:T(256)}, u32[]{:S(2)}) copy-start(f32[256]{0:T(256)} %param.12) | copy-start | bytes 3076
  29.4 3.5 %copy-start.2 = (bf16[3,256,256]{2,1,0:T(8,128)(2,1)S(1)}, bf16[3,256,256]{2,1,0:T(8,128)(2,1)}, u32[]{:S(2)}) copy-start(bf16[3,256,256]{2,1,0:T(8,128)(2,1)} %param.11) | copy-start | bytes 1179652
  30.7 27.4 %collective-permute-start.2 = (bf16[2,16,128,256]{3,2,1,0:T(8,128)(2,1)S(1)}, bf16[2,16,128,256]{3,2,1,0:T(8,128)(2,1)S(1)}, u32[]{:S(2)}, u32[]{:S(2)}) collective-permute-start(bf16[2,16,128,256]{3,2,1,0:T(8,128)(2,1)S(1)} %fusion.19), channel_id=1, source_target_pairs={{0,4},{4,8},{8,12},{1,5},{5,9},{9,13},{2,6},{6,10},{10,14},{3,7},{... | collective-permute-start | bytes 6291464 | tf_op jit(solution)/shard_map/ppermute | solution.py:23
  58.5 0.9 %copy-start.6 = (f32[256]{0:T(256)S(1)}, f32[256]{0:T(256)}, u32[]{:S(2)}) copy-start(f32[256]{0:T(256)} %param.13) | copy-start | bytes 3076
where the time goes:
time: 62 us; the launch traced here: 61.6 us
  waiting for transfers between devices  28.6 us (46%)
  other arithmetic  10.1 us (16%)
  matrix products  9.43 us (15%)
  starting transfers between devices  7.95 us (13%)
  local copies, waits for them, and re-layouts  5.29 us (9%)
    ppermute x1, waiting for transfers between devices, passed_along(): return lax.ppermute(array, axis, pairs)  24.1 us
    dot_general x9, matrix products, body(): jnp.dot(window, space_kernel[tap_row, tap_col], preferred_element_type=jn...  6.97 us
    slice x1, local copies, waits for them, and re-layouts, body(): padded[:, tap_row:tap_row + rows_count, tap_col:tap_col + cols_count]  5.21 us
    ppermute x1, starting transfers between devices, with_halo(): before = lax.ppermute(last, axis, up)  3.48 us
    ppermute x1, waiting for transfers between devices, with_halo(): after = lax.ppermute(first, axis, down)  3.22 us
    reduce_sum x2, other arithmetic, rms_silu(): jnp.mean(widened * widened, axis=-1, keepdims=True) + 1e-06  2.97 us
    convert_element_type x2, other arithmetic, rms_silu(): return jax.nn.silu(scaled).astype(jnp.bfloat16)  2.78 us
    dot_general x4, matrix products, lag_product(): jnp.dot(frames_in.reshape(-1, channels), kernel_slice, preferred_element_...  2.45 us
  transfers between devices with their start and end apart: 3, of which 3 were waited for; matrix products, arithmetic and copies ran while one was open for 2% of the time, Pallas kernels for 0%

commit v1 on v0

v1 whole, which is shorter than its diff:
```python
import functools

import jax
import jax.numpy as jnp
from jax import lax
from jax.experimental import pallas as pl
from jax.experimental.pallas import tpu as pltpu
from jax.sharding import PartitionSpec as P

LAGS = 2


def rms_silu(values, gain):
    mean = jnp.mean(values * values, axis=-1, keepdims=True)
    scaled = values * lax.rsqrt(mean + 1e-06) * gain
    return scaled / (1.0 + jnp.exp(-scaled))


def kernel(
    features, space_kernel, space_gain, space_bias, time_kernel, time_gain, time_bias,
    out,
    feat, normed, hidden, ntime, earlier, wspace, wtime, vectors,
    feat_sem, weight_sem, halo_send, halo_recv, time_send, time_recv,
):
    frames, rows, cols, channels = features.shape
    pixels = frames * cols
    band, bands = lax.axis_index("band"), lax.axis_size("band")
    frame, frame_parts = lax.axis_index("frame"), lax.axis_size("frame")
    has_up, has_down = band > 0, band < bands - 1
    has_prev, has_next = frame > 0, frame < frame_parts - 1
    neighbours = (
        (has_up, {"band": band - 1}),
        (has_down, {"band": band + 1}),
        (has_prev, {"frame": frame - 1}),
        (has_next, {"frame": frame + 1}),
    )

    barrier = pltpu.get_barrier_semaphore()
    for present, device in neighbours:
        @pl.when(present)
        def _():
            pl.semaphore_signal(
                barrier, inc=1, device_id=device, device_id_type=pl.DeviceIdType.MESH
            )

    def row_copy(row):
        return pltpu.make_async_copy(
            features.at[:, row], feat.at[row + 1], feat_sem.at[row]
        )

    weights = [(space_kernel, wspace), (time_kernel, wtime)] + [
        (vector, vectors.at[i])
        for i, vector in enumerate((space_gain, space_bias, time_gain, time_bias))
    ]
    weight_copies = [
        pltpu.make_async_copy(source, target, weight_sem.at[i])
        for i, (source, target) in enumerate(weights)
    ]
    for i in (2, 3, 4, 5):
        weight_copies[i].start()
    for row in range(min(3, rows)):
        row_copy(row).start()
    weight_copies[0].start()
    for row in range(3, rows):
        row_copy(row).start()
    weight_copies[1].start()

    peers = (
        (band + bands - 1) // bands
        + 1 - (band + 1) // bands
        + (frame + frame_parts - 1) // frame_parts
        + 1 - (frame + 1) // frame_parts
    )
    pl.semaphore_wait(barrier, peers)

    to_up = pltpu.make_async_remote_copy(
        features.at[:, 0], feat.at[rows + 1], halo_send.at[0], halo_recv.at[0],
        device_id={"band": band - 1}, device_id_type=pl.DeviceIdType.MESH,
    )
    to_down = pltpu.make_async_remote_copy(
        features.at[:, rows - 1], feat.at[0], halo_send.at[1], halo_recv.at[1],
        device_id={"band": band + 1}, device_id_type=pl.DeviceIdType.MESH,
    )
    pl.when(has_up)(to_up.start)
    pl.when(has_down)(to_down.start)

    def time_copy(row):
        return pltpu.make_async_remote_copy(
            ntime.at[row, pl.ds(pixels - LAGS * cols, LAGS * cols)],
            earlier.at[row],
            time_send.at[row],
            time_recv.at[row],
            device_id={"frame": frame + 1},
            device_id_type=pl.DeviceIdType.MESH,
        )

    column = lax.rem(lax.broadcasted_iota(jnp.int32, (pixels, channels), 0), cols)

    def vector(i):
        return vectors[i].reshape(1, channels)

    def norm_row(slot):
        values = feat[slot].reshape(pixels, channels).astype(jnp.float32)
        result = rms_silu(values, vector(0))
        left = jnp.where(column == 0, 0.0, pltpu.roll(result, 1, 0))
        right = jnp.where(column == cols - 1, 0.0, pltpu.roll(result, pixels - 1, 0))
        normed[slot, :, :channels] = left.astype(jnp.bfloat16)
        normed[slot, :, channels : 2 * channels] = result.astype(jnp.bfloat16)
        normed[slot, :, 2 * channels :] = right.astype(jnp.bfloat16)

    def space_row(row):
        total = None
        for i in range(3):
            product = jnp.dot(
                normed[row + i],
                wspace[i].reshape(3 * channels, channels),
                preferred_element_type=jnp.float32,
            )
            total = product if total is None else total + product
        centre = feat[row + 1].reshape(pixels, channels).astype(jnp.float32)
        kept = (centre + total + vector(1)).astype(jnp.bfloat16)
        hidden[row] = kept
        ntime[row] = rms_silu(kept.astype(jnp.float32), vector(2)).astype(jnp.bfloat16)

        @pl.when(has_next)
        def _():
            time_copy(row).start()

    def time_row(row):
        pl.when(has_prev)(time_copy(row).wait_recv)
        own = ntime[row]
        window = jnp.concatenate([earlier[row], own], axis=0)
        total = jnp.dot(own, wtime[0], preferred_element_type=jnp.float32)
        for lag in range(1, LAGS + 1):
            start = (LAGS - lag) * cols
            total = total + jnp.dot(
                window[start : start + pixels], wtime[lag],
                preferred_element_type=jnp.float32,
            )
        temporal = total.astype(jnp.bfloat16).astype(jnp.float32)
        decoded = hidden[row].astype(jnp.float32) + temporal + vector(3)
        out[:, row] = decoded.astype(jnp.bfloat16).reshape(frames, cols, channels)

    @pl.when(jnp.logical_not(has_prev))
    def _():
        earlier[...] = jnp.zeros_like(earlier)

    @pl.when(jnp.logical_not(has_up))
    def _():
        feat[0] = jnp.zeros(feat.shape[1:], feat.dtype)

    @pl.when(jnp.logical_not(has_down))
    def _():
        feat[rows + 1] = jnp.zeros(feat.shape[1:], feat.dtype)

    for i in (2, 3, 4, 5):
        weight_copies[i].wait()

    @pl.loop(0, 2)
    def _(row):
        row_copy(row).wait()
        norm_row(row + 1)

    row_copy(2).wait()
    norm_row(3)
    weight_copies[0].wait()
    space_row(1)

    @pl.loop(2, rows - 1)
    def _(row):
        row_copy(row + 1).wait()
        norm_row(row + 2)
        space_row(row)

    pl.when(has_up)(to_down.wait_recv)
    pl.when(has_down)(to_up.wait_recv)

    @pl.loop(0, 2)
    def _(side):
        norm_row(side * (rows + 1))
        space_row(side * (rows - 1))

    weight_copies[1].wait()

    @pl.loop(1, rows + 1)
    def _(step):
        time_row(order(step, rows))

    pl.when(has_up)(to_up.wait_send)
    pl.when(has_down)(to_down.wait_send)

    @pl.when(has_next)
    def _():
        @pl.loop(0, rows)
        def _(row):
            time_copy(row).wait_send()


def order(step, rows):
    late = step // (rows - 1)
    last = step // rows
    return step * (1 - late) + last * (rows - 1)


def body(features, *rest):
    frames, rows, cols, channels = features.shape
    pixels = frames * cols
    bf16 = jnp.bfloat16
    return pl.pallas_call(
        kernel,
        out_shape=jax.ShapeDtypeStruct(features.shape, bf16),
        in_specs=[pl.BlockSpec(memory_space=pltpu.HBM)] * 7,
        out_specs=pl.BlockSpec(memory_space=pltpu.VMEM),
        scratch_shapes=[
            pltpu.VMEM((rows + 2, frames, cols, channels), bf16),
            pltpu.VMEM((rows + 2, pixels, 3 * channels), bf16),
            pltpu.VMEM((rows, pixels, channels), bf16),
            pltpu.VMEM((rows, pixels, channels), bf16),
            pltpu.VMEM((rows, LAGS * cols, channels), bf16),
            pltpu.VMEM(rest[0].shape, bf16),
            pltpu.VMEM(rest[3].shape, bf16),
            pltpu.VMEM((4, channels), jnp.float32),
            pltpu.SemaphoreType.DMA((rows,)),
            pltpu.SemaphoreType.DMA((6,)),
            pltpu.SemaphoreType.DMA((2,)),
            pltpu.SemaphoreType.DMA((2,)),
            pltpu.SemaphoreType.DMA((rows,)),
            pltpu.SemaphoreType.DMA((rows,)),
        ],
        compiler_params=pltpu.CompilerParams(
            collective_id=0, has_side_effects=True, vmem_limit_bytes=36 * 1024 * 1024
        ),
    )(features, *rest)


def solution(mesh):
    return jax.shard_map(
        body,
        mesh=mesh,
        in_specs=(P(("grp", "frame"), "band", None, None), P(), P(), P(), P(), P(), P()),
        out_specs=P(("grp", "frame"), "band", None, None),
        check_vma=False,
    )
```

time: 62 us -> 36 us (0.58)
  waiting for transfers between devices: 28.6 us -> 0 us
  Pallas kernels: 0 us -> 27.8 us
  other arithmetic: 10.1 us -> 0 us
  matrix products: 9.43 us -> 0 us
  starting transfers between devices: 7.95 us -> 0 us
  local copies, waits for them, and re-layouts: 5.29 us -> 7.89 us
    ppermute x3 -> x0, waiting for transfers between devices: 28.6 us -> none  [the longest x1 24.1 us: passed_along(): return lax.ppermute(array, axis, pairs)]
    pallas_call x0 -> x1, Pallas kernels: none -> 27.8 us  [body(): pl.pallas_call(kernel, out_shape=jax.ShapeDtypeStruct(features.shape, bf1...]
    dot_general x13 -> x0, matrix products: 9.43 us -> none  [the longest x9 6.97 us: body(): jnp.dot(window, space_kernel[tap_row, tap_col], preferred_element_type=jn...]
    ppermute x3 -> x0, starting transfers between devices: 7.95 us -> none  [the longest x1 3.48 us: with_halo(): before = lax.ppermute(last, axis, up)]
    unnamed x14 -> x15, local copies, waits for them, and re-layouts: 0.07 us -> 7.89 us
    convert_element_type x4 -> x0, other arithmetic: 5.81 us -> none  [the longest x2 2.78 us: rms_silu(): return jax.nn.silu(scaled).astype(jnp.bfloat16)]
    slice x2 -> x0, local copies, waits for them, and re-layouts: 5.23 us -> none  [the longest x1 5.21 us: body(): padded[:, tap_row:tap_row + rows_count, tap_col:tap_col + cols_count]]
    reduce_sum x2 -> x0, other arithmetic: 2.97 us -> none  [rms_silu(): jnp.mean(widened * widened, axis=-1, keepdims=True) + 1e-06]
  transfers between devices with their start and end apart: 3 -> 0, of which waited for: 3 -> 0; matrix products, arithmetic and copies ran while one was open for 2% -> 0% of each run, Pallas kernels for 0% -> 0%
where the time goes in v1:
time: 36 us; the launch traced here: 35.7 us
  Pallas kernels  27.8 us (77%)
  local copies, waits for them, and re-layouts  7.89 us (22%)
    pallas_call x1, Pallas kernels, body(): pl.pallas_call(kernel, out_shape=jax.ShapeDtypeStruct(features.shape, bf1...  27.8 us
    unnamed x15, local copies, waits for them, and re-layouts  7.89 us

profile of v1, /device:TPU:14, one launch (start us, length us, event | category | flops | bytes accessed | tf_op | source)
XLA Modules:
  0.0 35.7 jit_solution(1159384749149229308)
XLA Ops:
  0.0 0.0 copy-start
  0.0 1.6 %copy-done = bf16[2,16,128,256]{3,2,1,0:T(8,128)(2,1)S(1)} copy-done((bf16[2,16,128,256]{3,2,1,0:T(8,128)(2,1)S(1)}, bf16[2,16,128,256]{3,2,1,0:T(8,128)(2,1)}, u32[]{:S(2)}) %copy-start) | copy-done | bytes 2097176
  1.6 0.0 copy-start.1
  1.6 1.3 %copy-done.1 = bf16[3,3,256,256]{3,2,1,0:T(8,128)(2,1)S(1)} copy-done((bf16[3,3,256,256]{3,2,1,0:T(8,128)(2,1)S(1)}, bf16[3,3,256,256]{3,2,1,0:T(8,128)(2,1)}, u32[]{:S(2)}) %copy-start.1) | copy-done | bytes 1179672
  2.9 0.0 copy-start.2
  2.9 1.0 %copy-done.2 = bf16[3,256,256]{2,1,0:T(8,128)(2,1)S(1)} copy-done((bf16[3,256,256]{2,1,0:T(8,128)(2,1)S(1)}, bf16[3,256,256]{2,1,0:T(8,128)(2,1)}, u32[]{:S(2)}) %copy-start.2) | copy-done | bytes 393240
  3.9 0.0 copy-start.3
  3.9 0.7 %copy-done.3 = f32[256]{0:T(256)S(1)} copy-done((f32[256]{0:T(256)S(1)}, f32[256]{0:T(256)}, u32[]{:S(2)}) %copy-start.3) | copy-done | bytes 1048
  4.5 0.0 copy-start.4
  4.5 0.7 %copy-done.4 = f32[256]{0:T(256)S(1)} copy-done((f32[256]{0:T(256)S(1)}, f32[256]{0:T(256)}, u32[]{:S(2)}) %copy-start.4) | copy-done | bytes 1048
  5.2 0.0 copy-start.5
  5.2 0.7 %copy-done.5 = f32[256]{0:T(256)S(1)} copy-done((f32[256]{0:T(256)S(1)}, f32[256]{0:T(256)}, u32[]{:S(2)}) %copy-start.5) | copy-done | bytes 1048
  5.9 0.0 copy-start.6
  5.9 0.7 %copy-done.6 = f32[256]{0:T(256)S(1)} copy-done((f32[256]{0:T(256)S(1)}, f32[256]{0:T(256)}, u32[]{:S(2)}) %copy-start.6) | copy-done | bytes 1048
  6.6 27.8 %shard_map.73 = bf16[2,16,128,256]{3,2,1,0:T(8,128)(2,1)S(1)} custom-call(bf16[2,16,128,256]{3,2,1,0:T(8,128)(2,1)S(1)} %copy-done, bf16[3,3,256,256]{3,2,1,0:T(8,128)(2,1)S(1)} %copy-done.1, f32[256]{0:T(256)S(1)} %copy-done.3, f32[256]{0:T(256)S(1)} %copy-done.4, bf16[3,256,256]{2,1,0:T(8,128)(2,1)S(1)} %copy-done.2, f32[256]{0:T(256)S(1)} %copy-done.5, ...), custom_call_target="tpu_custom_call" | custom-call | tf_op jit(solution)/shard_map/pallas_call | solution.py:209
  34.4 1.3 %copy.9 = bf16[2,16,128,256]{3,2,1,0:T(8,128)(2,1)} copy(bf16[2,16,128,256]{3,2,1,0:T(8,128)(2,1)S(1)} %shard_map.73) | data formatting | bytes 4194304
Async XLA Ops:
  0.0 1.6 %copy-start = (bf16[2,16,128,256]{3,2,1,0:T(8,128)(2,1)S(1)}, bf16[2,16,128,256]{3,2,1,0:T(8,128)(2,1)}, u32[]{:S(2)}) copy-start(bf16[2,16,128,256]{3,2,1,0:T(8,128)(2,1)} %features.1) | copy-start | bytes 6291460
  1.6 1.3 %copy-start.1 = (bf16[3,3,256,256]{3,2,1,0:T(8,128)(2,1)S(1)}, bf16[3,3,256,256]{3,2,1,0:T(8,128)(2,1)}, u32[]{:S(2)}) copy-start(bf16[3,3,256,256]{3,2,1,0:T(8,128)(2,1)} %space_kernel.1) | copy-start | bytes 3538948
  2.9 1.0 %copy-start.2 = (bf16[3,256,256]{2,1,0:T(8,128)(2,1)S(1)}, bf16[3,256,256]{2,1,0:T(8,128)(2,1)}, u32[]{:S(2)}) copy-start(bf16[3,256,256]{2,1,0:T(8,128)(2,1)} %time_kernel.1) | copy-start | bytes 1179652
  3.9 0.7 %copy-start.3 = (f32[256]{0:T(256)S(1)}, f32[256]{0:T(256)}, u32[]{:S(2)}) copy-start(f32[256]{0:T(256)} %space_gain.1) | copy-start | bytes 3076
  4.5 0.7 %copy-start.4 = (f32[256]{0:T(256)S(1)}, f32[256]{0:T(256)}, u32[]{:S(2)}) copy-start(f32[256]{0:T(256)} %space_bias.1) | copy-start | bytes 3076
  5.2 0.7 %copy-start.5 = (f32[256]{0:T(256)S(1)}, f32[256]{0:T(256)}, u32[]{:S(2)}) copy-start(f32[256]{0:T(256)} %time_gain.1) | copy-start | bytes 3076
  5.9 0.7 %copy-start.6 = (f32[256]{0:T(256)S(1)}, f32[256]{0:T(256)}, u32[]{:S(2)}) copy-start(f32[256]{0:T(256)} %time_bias.1) | copy-start | bytes 3076

commit v2 on v1

--- a/solution.py
+++ b/solution.py
@@ -230,7 +230,7 @@
         compiler_params=pltpu.CompilerParams(
             collective_id=0, has_side_effects=True, vmem_limit_bytes=36 * 1024 * 1024
         ),
-    )(features, *rest)
+    )(*[pltpu.with_memory_space_constraint(x, pltpu.HBM) for x in (features, *rest)])
 
 
 def solution(mesh):

time: 36 us -> 29.2 us (0.81)
  local copies, waits for them, and re-layouts: 7.89 us -> 1.32 us
    unnamed x15 -> x1, local copies, waits for them, and re-layouts: 7.89 us -> 1.32 us
where the time goes in v2:
time: 29.2 us; the launch traced here: 29 us
  Pallas kernels  27.7 us (95%)
  local copies, waits for them, and re-layouts  1.32 us (5%)
    pallas_call x1, Pallas kernels, body(): pl.pallas_call(kernel, out_shape=jax.ShapeDtypeStruct(features.shape, bf1...  27.7 us
    unnamed x1, local copies, waits for them, and re-layouts  1.32 us

profile of v2, /device:TPU:14, one launch (start us, length us, event | category | flops | bytes accessed | tf_op | source)
XLA Modules:
  0.0 29.0 jit_solution(7668572848290238566)
XLA Ops:
  0.0 27.7 %shard_map.73 = bf16[2,16,128,256]{3,2,1,0:T(8,128)(2,1)S(1)} custom-call(bf16[2,16,128,256]{3,2,1,0:T(8,128)(2,1)} %features.1, bf16[3,3,256,256]{3,2,1,0:T(8,128)(2,1)} %space_kernel.1, f32[256]{0:T(256)} %space_gain.1, f32[256]{0:T(256)} %space_bias.1, bf16[3,256,256]{2,1,0:T(8,128)(2,1)} %time_kernel.1, f32[256]{0:T(256)} %time_gain.1, f32[256]{0:T(256)} %time_bias.1), custom_call_target="tpu_custom_call" | custom-call | tf_op jit(solution)/shard_map/pallas_call | solution.py:209
  27.7 1.3 %copy.9 = bf16[2,16,128,256]{3,2,1,0:T(8,128)(2,1)} copy(bf16[2,16,128,256]{3,2,1,0:T(8,128)(2,1)S(1)} %shard_map.73) | data formatting | bytes 4194304

commit v3 on v2

v3 whole, which is shorter than its diff:
```python
import functools

import jax
import jax.numpy as jnp
from jax import lax
from jax.experimental import pallas as pl
from jax.experimental.pallas import tpu as pltpu
from jax.sharding import PartitionSpec as P

LAGS = 2


def rms_silu(values, gain):
    mean = jnp.mean(values * values, axis=-1, keepdims=True)
    half = values * lax.rsqrt(mean + 1e-06) * (0.5 * gain)
    return half + half * jnp.tanh(half)


def dot(left, right):
    return jnp.dot(left, right, preferred_element_type=jnp.float32)


def kernel(
    features, space_kernel, space_gain, space_bias, time_kernel, time_gain, time_bias,
    out,
    feat, normed, hidden, ntime, earlier, wspace, wtime, vectors,
    feat_sem, weight_sem, halo_send, halo_recv, time_send, time_recv,
):
    frames, rows, cols, channels = features.shape
    half = cols // 2
    first, last = 1, rows - 1
    band, bands = lax.axis_index("band"), lax.axis_size("band")
    frame, frame_parts = lax.axis_index("frame"), lax.axis_size("frame")
    has_up, has_down = band > 0, band < bands - 1
    has_prev, has_next = frame > 0, frame < frame_parts - 1
    neighbours = (
        (has_up, {"band": band - 1}),
        (has_down, {"band": band + 1}),
        (has_prev, {"frame": frame - 1}),
        (has_next, {"frame": frame + 1}),
    )

    barrier = pltpu.get_barrier_semaphore()
    for present, device in neighbours:
        @pl.when(present)
        def _():
            pl.semaphore_signal(
                barrier, inc=1, device_id=device, device_id_type=pl.DeviceIdType.MESH
            )

    def row_copy(row):
        return pltpu.make_async_copy(
            features.at[:, row], feat.at[row + 1], feat_sem.at[row]
        )

    weights = [(space_kernel, wspace), (time_kernel, wtime)] + [
        (vector, vectors.at[i])
        for i, vector in enumerate((space_gain, space_bias, time_gain, time_bias))
    ]
    weight_copies = [
        pltpu.make_async_copy(source, target, weight_sem.at[i])
        for i, (source, target) in enumerate(weights)
    ]
    for i in (2, 3, 4, 5):
        weight_copies[i].start()
    for row in range(3):
        row_copy(row).start()
    weight_copies[0].start()
    for row in range(3, rows):
        row_copy(row).start()
    weight_copies[1].start()

    peers = (
        (band + bands - 1) // bands
        + 1 - (band + 1) // bands
        + (frame + frame_parts - 1) // frame_parts
        + 1 - (frame + 1) // frame_parts
    )
    pl.semaphore_wait(barrier, peers)

    to_up = pltpu.make_async_remote_copy(
        features.at[:, 0], feat.at[rows + 1], halo_send.at[0], halo_recv.at[0],
        device_id={"band": band - 1}, device_id_type=pl.DeviceIdType.MESH,
    )
    to_down = pltpu.make_async_remote_copy(
        features.at[:, rows - 1], feat.at[0], halo_send.at[1], halo_recv.at[1],
        device_id={"band": band + 1}, device_id_type=pl.DeviceIdType.MESH,
    )
    pl.when(has_up)(to_up.start)
    pl.when(has_down)(to_down.start)

    def time_copy(row, sem, start=0, count=LAGS, left=0, width=cols):
        return pltpu.make_async_remote_copy(
            ntime.at[row, pl.ds(frames - LAGS + start, count), pl.ds(left, width)],
            earlier.at[row, pl.ds(start, count), pl.ds(left, width)],
            time_send.at[sem],
            time_recv.at[sem],
            device_id={"frame": frame + 1},
            device_id_type=pl.DeviceIdType.MESH,
        )

    first_copies = {
        (start, side): time_copy(first, rows + 2 * start + side, start, 1, side * half, half)
        for start in range(LAGS)
        for side in range(2)
    }
    last_copies = [
        time_copy(last, rows + 2 * LAGS + side, 0, LAGS, side * half, half)
        for side in range(2)
    ]

    def vector(i):
        return vectors[i].reshape(1, channels)

    def norm_part(slot, start=0, count=frames, left=0, width=cols):
        base = max(0, min(left - 16, cols - width - 16)) if width < cols else 0
        window = min(cols, width + 16)
        size = count * window
        values = feat[slot, start : start + count, base : base + window]
        result = rms_silu(values.reshape(size, channels).astype(jnp.float32), vector(0))
        column = base + lax.rem(
            lax.broadcasted_iota(jnp.int32, (size, channels), 0), window
        )
        before = jnp.where(column == 0, 0.0, pltpu.roll(result, 1, 0))
        after = jnp.where(column == cols - 1, 0.0, pltpu.roll(result, size - 1, 0))
        for i, piece in enumerate((before, result, after)):
            kept = piece.astype(jnp.bfloat16).reshape(count, window, channels)
            normed[
                slot, start : start + count, left : left + width,
                i * channels : (i + 1) * channels,
            ] = kept[:, left - base : left - base + width]

    def space_part(row, start=0, count=frames, left=0, width=cols):
        where = (slice(start, start + count), slice(left, left + width))
        size = count * width
        total = None
        for i in range(3):
            product = dot(
                normed[(row + i, *where)].reshape(size, 3 * channels),
                wspace[i].reshape(3 * channels, channels),
            )
            total = product if total is None else total + product
        centre = feat[(row + 1, *where)].reshape(size, channels).astype(jnp.float32)
        kept = (centre + total + vector(1)).astype(jnp.bfloat16)
        shape = (count, width, channels)
        hidden[(row, *where)] = kept.reshape(shape)
        ntime[(row, *where)] = (
            rms_silu(kept.astype(jnp.float32), vector(2)).astype(jnp.bfloat16).reshape(shape)
        )

    def space_row(row):
        space_part(row)
        pl.when(has_next)(time_copy(row, row).start)

    def time_part(row, copies, left=0, width=cols):
        columns = slice(left, left + width)
        own = ntime[row, :, columns]
        totals = [
            dot(own.reshape(-1, channels), wtime[0]).reshape(own.shape)[f]
            for f in range(frames)
        ]
        for lag in range(1, min(LAGS, frames - 1) + 1):
            term = dot(own[: frames - lag].reshape(-1, channels), wtime[lag])
            for f in range(lag, frames):
                totals[f] += term[(f - lag) * width : (f - lag + 1) * width]

        @pl.when(has_prev)
        def _():
            for copy in copies:
                copy.wait_recv()

        for lag in range(1, LAGS + 1):
            count = min(lag, frames)
            past = earlier[row, LAGS - lag : LAGS - lag + count, columns]
            term = dot(past.reshape(-1, channels), wtime[lag])
            for f in range(count):
                totals[f] += term[f * width : (f + 1) * width]
        for f in range(frames):
            temporal = totals[f].astype(jnp.bfloat16).astype(jnp.float32)
            kept = hidden[row, f, columns].astype(jnp.float32)
            out[f, row, columns] = (kept + temporal + vector(3)).astype(jnp.bfloat16)

    @pl.when(jnp.logical_not(has_prev))
    def _():
        earlier[...] = jnp.zeros_like(earlier)

    @pl.when(jnp.logical_not(has_up))
    def _():
        feat[0] = jnp.zeros(feat.shape[1:], feat.dtype)

    @pl.when(jnp.logical_not(has_down))
    def _():
        feat[rows + 1] = jnp.zeros(feat.shape[1:], feat.dtype)

    for i in (2, 3, 4, 5):
        weight_copies[i].wait()
    for row in range(3):
        row_copy(row).wait()
    for f in reversed(range(frames)):
        for side in range(2):
            part = (f, 1, side * half, half)
            for slot in range(first, first + 3):
                norm_part(slot, *part)
            if f == frames - 1 and side == 0:
                weight_copies[0].wait()
            space_part(first, *part)
            if f >= frames - LAGS:
                pl.when(has_next)(first_copies[f - frames + LAGS, side].start)

    @pl.loop(first + 1, last)
    def _(row):
        row_copy(row + 1).wait()
        norm_part(row + 2)
        space_row(row)

    pl.when(has_up)(to_down.wait_recv)
    pl.when(has_down)(to_up.wait_recv)
    norm_part(0)
    space_row(0)
    norm_part(rows + 1)
    space_part(last)

    @pl.when(has_next)
    def _():
        for copy in last_copies:
            copy.start()

    weight_copies[1].wait()
    time_part(first, first_copies.values())

    @pl.loop(first + 1, last)
    def _(row):
        time_part(row, [time_copy(row, row)])

    time_part(0, [time_copy(0, 0)])
    for side in range(2):
        time_part(last, [last_copies[side]], side * half, half)

    pl.when(has_up)(to_up.wait_send)
    pl.when(has_down)(to_down.wait_send)

    @pl.when(has_next)
    def _():
        for copy in (time_copy(0, 0), *first_copies.values(), *last_copies):
            copy.wait_send()

        @pl.loop(first + 1, last)
        def _(row):
            time_copy(row, row).wait_send()


def body(features, *rest):
    frames, rows, cols, channels = features.shape
    bf16 = jnp.bfloat16
    return pl.pallas_call(
        kernel,
        out_shape=jax.ShapeDtypeStruct(features.shape, bf16),
        in_specs=[pl.BlockSpec(memory_space=pltpu.HBM)] * 7,
        out_specs=pl.BlockSpec(memory_space=pltpu.VMEM),
        scratch_shapes=[
            pltpu.VMEM((rows + 2, frames, cols, channels), bf16),
            pltpu.VMEM((rows + 2, frames, cols, 3 * channels), bf16),
            pltpu.VMEM((rows, frames, cols, channels), bf16),
            pltpu.VMEM((rows, frames, cols, channels), bf16),
            pltpu.VMEM((rows, LAGS, cols, channels), bf16),
            pltpu.VMEM(rest[0].shape, bf16),
            pltpu.VMEM(rest[3].shape, bf16),
            pltpu.VMEM((4, channels), jnp.float32),
            pltpu.SemaphoreType.DMA((rows,)),
            pltpu.SemaphoreType.DMA((6,)),
            pltpu.SemaphoreType.DMA((2,)),
            pltpu.SemaphoreType.DMA((2,)),
            pltpu.SemaphoreType.DMA((rows + 2 * LAGS + 2,)),
            pltpu.SemaphoreType.DMA((rows + 2 * LAGS + 2,)),
        ],
        compiler_params=pltpu.CompilerParams(
            collective_id=0, has_side_effects=True, vmem_limit_bytes=36 * 1024 * 1024
        ),
    )(*[pltpu.with_memory_space_constraint(x, pltpu.HBM) for x in (features, *rest)])


def solution(mesh):
    return jax.shard_map(
        body,
        mesh=mesh,
        in_specs=(P(("grp", "frame"), "band", None, None), P(), P(), P(), P(), P(), P()),
        out_specs=P(("grp", "frame"), "band", None, None),
        check_vma=False,
    )
```

time: 29.2 us -> 29.8 us (1.021)
  Pallas kernels: 27.7 us -> 28.3 us
    pallas_call x1, Pallas kernels: 27.7 us -> 28.3 us  [body(): pl.pallas_call(kernel, out_shape=jax.ShapeDtypeStruct(features.shape, bf1...]
where the time goes in v3:
time: 29.8 us; the launch traced here: 29.6 us
  Pallas kernels  28.3 us (95%)
  local copies, waits for them, and re-layouts  1.32 us (4%)
    pallas_call x1, Pallas kernels, body(): pl.pallas_call(kernel, out_shape=jax.ShapeDtypeStruct(features.shape, bf1...  28.3 us
    unnamed x1, local copies, waits for them, and re-layouts  1.32 us

profile of v3, /device:TPU:14, one launch (start us, length us, event | category | flops | bytes accessed | tf_op | source)
XLA Modules:
  0.0 29.6 jit_solution(5664142804479107891)
XLA Ops:
  0.0 28.3 %shard_map.73 = bf16[2,16,128,256]{3,2,1,0:T(8,128)(2,1)S(1)} custom-call(bf16[2,16,128,256]{3,2,1,0:T(8,128)(2,1)} %features.1, bf16[3,3,256,256]{3,2,1,0:T(8,128)(2,1)} %space_kernel.1, f32[256]{0:T(256)} %space_gain.1, f32[256]{0:T(256)} %space_bias.1, bf16[3,256,256]{2,1,0:T(8,128)(2,1)} %time_kernel.1, f32[256]{0:T(256)} %time_gain.1, f32[256]{0:T(256)} %time_bias.1), custom_call_target="tpu_custom_call" | custom-call | tf_op jit(solution)/shard_map/pallas_call | solution.py:255
  28.3 1.3 %copy.9 = bf16[2,16,128,256]{3,2,1,0:T(8,128)(2,1)} copy(bf16[2,16,128,256]{3,2,1,0:T(8,128)(2,1)S(1)} %shard_map.73) | data formatting | bytes 4194304

commit v4 on v3

--- a/solution.py
+++ b/solution.py
@@ -28,7 +28,7 @@
 ):
     frames, rows, cols, channels = features.shape
     half = cols // 2
-    first, last = 1, rows - 1
+    last = rows - 1
     band, bands = lax.axis_index("band"), lax.axis_size("band")
     frame, frame_parts = lax.axis_index("frame"), lax.axis_size("frame")
     has_up, has_down = band > 0, band < bands - 1
@@ -70,25 +70,6 @@
         row_copy(row).start()
     weight_copies[1].start()
 
-    peers = (
-        (band + bands - 1) // bands
-        + 1 - (band + 1) // bands
-        + (frame + frame_parts - 1) // frame_parts
-        + 1 - (frame + 1) // frame_parts
-    )
-    pl.semaphore_wait(barrier, peers)
-
-    to_up = pltpu.make_async_remote_copy(
-        features.at[:, 0], feat.at[rows + 1], halo_send.at[0], halo_recv.at[0],
-        device_id={"band": band - 1}, device_id_type=pl.DeviceIdType.MESH,
-    )
-    to_down = pltpu.make_async_remote_copy(
-        features.at[:, rows - 1], feat.at[0], halo_send.at[1], halo_recv.at[1],
-        device_id={"band": band + 1}, device_id_type=pl.DeviceIdType.MESH,
-    )
-    pl.when(has_up)(to_up.start)
-    pl.when(has_down)(to_down.start)
-
     def time_copy(row, sem, start=0, count=LAGS, left=0, width=cols):
         return pltpu.make_async_remote_copy(
             ntime.at[row, pl.ds(frames - LAGS + start, count), pl.ds(left, width)],
@@ -99,13 +80,8 @@
             device_id_type=pl.DeviceIdType.MESH,
         )
 
-    first_copies = {
-        (start, side): time_copy(first, rows + 2 * start + side, start, 1, side * half, half)
-        for start in range(LAGS)
-        for side in range(2)
-    }
     last_copies = [
-        time_copy(last, rows + 2 * LAGS + side, 0, LAGS, side * half, half)
+        time_copy(last, rows + side, 0, LAGS, side * half, half)
         for side in range(2)
     ]
 
@@ -196,18 +172,31 @@
         weight_copies[i].wait()
     for row in range(3):
         row_copy(row).wait()
-    for f in reversed(range(frames)):
-        for side in range(2):
-            part = (f, 1, side * half, half)
-            for slot in range(first, first + 3):
-                norm_part(slot, *part)
-            if f == frames - 1 and side == 0:
-                weight_copies[0].wait()
-            space_part(first, *part)
-            if f >= frames - LAGS:
-                pl.when(has_next)(first_copies[f - frames + LAGS, side].start)
-
-    @pl.loop(first + 1, last)
+        norm_part(row + 1)
+
+    peers = (
+        (band + bands - 1) // bands
+        + 1 - (band + 1) // bands
+        + (frame + frame_parts - 1) // frame_parts
+        + 1 - (frame + 1) // frame_parts
+    )
+    pl.semaphore_wait(barrier, peers)
+
+    to_up = pltpu.make_async_remote_copy(
+        features.at[:, 0], feat.at[rows + 1], halo_send.at[0], halo_recv.at[0],
+        device_id={"band": band - 1}, device_id_type=pl.DeviceIdType.MESH,
+    )
+    to_down = pltpu.make_async_remote_copy(
+        features.at[:, rows - 1], feat.at[0], halo_send.at[1], halo_recv.at[1],
+        device_id={"band": band + 1}, device_id_type=pl.DeviceIdType.MESH,
+    )
+    pl.when(has_up)(to_up.start)
+    pl.when(has_down)(to_down.start)
+
+    weight_copies[0].wait()
+    space_row(1)
+
+    @pl.loop(2, last)
     def _(row):
         row_copy(row + 1).wait()
         norm_part(row + 2)
@@ -226,9 +215,7 @@
             copy.start()
 
     weight_copies[1].wait()
-    time_part(first, first_copies.values())
-
-    @pl.loop(first + 1, last)
+    @pl.loop(1, last)
     def _(row):
         time_part(row, [time_copy(row, row)])
 
@@ -241,10 +228,10 @@
 
     @pl.when(has_next)
     def _():
-        for copy in (time_copy(0, 0), *first_copies.values(), *last_copies):
+        for copy in (time_copy(0, 0), *last_copies):
             copy.wait_send()
 
-        @pl.loop(first + 1, last)
+        @pl.loop(1, last)
         def _(row):
             time_copy(row, row).wait_send()
 
@@ -270,8 +257,8 @@
             pltpu.SemaphoreType.DMA((6,)),
             pltpu.SemaphoreType.DMA((2,)),
             pltpu.SemaphoreType.DMA((2,)),
-            pltpu.SemaphoreType.DMA((rows + 2 * LAGS + 2,)),
-            pltpu.SemaphoreType.DMA((rows + 2 * LAGS + 2,)),
+            pltpu.SemaphoreType.DMA((rows + 2,)),
+            pltpu.SemaphoreType.DMA((rows + 2,)),
         ],
         compiler_params=pltpu.CompilerParams(
             collective_id=0, has_side_effects=True, vmem_limit_bytes=36 * 1024 * 1024

time: 29.8 us -> 28.6 us (0.960)
  Pallas kernels: 28.3 us -> 27.1 us
    pallas_call x1, Pallas kernels: 28.3 us -> 27.1 us  [body(): pl.pallas_call(kernel, out_shape=jax.ShapeDtypeStruct(features.shape, bf1...]
where the time goes in v4:
time: 28.6 us; the launch traced here: 28.4 us
  Pallas kernels  27.1 us (95%)
  local copies, waits for them, and re-layouts  1.32 us (5%)
    pallas_call x1, Pallas kernels, body(): pl.pallas_call(kernel, out_shape=jax.ShapeDtypeStruct(features.shape, bf1...  27.1 us
    unnamed x1, local copies, waits for them, and re-layouts  1.32 us

profile of v4, /device:TPU:14, one launch (start us, length us, event | category | flops | bytes accessed | tf_op | source)
XLA Modules:
  0.0 28.4 jit_solution(427332739419057873)
XLA Ops:
  0.0 27.1 %shard_map.73 = bf16[2,16,128,256]{3,2,1,0:T(8,128)(2,1)S(1)} custom-call(bf16[2,16,128,256]{3,2,1,0:T(8,128)(2,1)} %features.1, bf16[3,3,256,256]{3,2,1,0:T(8,128)(2,1)} %space_kernel.1, f32[256]{0:T(256)} %space_gain.1, f32[256]{0:T(256)} %space_bias.1, bf16[3,256,256]{2,1,0:T(8,128)(2,1)} %time_kernel.1, f32[256]{0:T(256)} %time_gain.1, f32[256]{0:T(256)} %time_bias.1), custom_call_target="tpu_custom_call" | custom-call | tf_op jit(solution)/shard_map/pallas_call | solution.py:242
  27.1 1.3 %copy.9 = bf16[2,16,128,256]{3,2,1,0:T(8,128)(2,1)} copy(bf16[2,16,128,256]{3,2,1,0:T(8,128)(2,1)S(1)} %shard_map.73) | data formatting | bytes 4194304

commit v5 on v4

--- a/solution.py
+++ b/solution.py
@@ -66,9 +66,6 @@
     for row in range(3):
         row_copy(row).start()
     weight_copies[0].start()
-    for row in range(3, rows):
-        row_copy(row).start()
-    weight_copies[1].start()
 
     def time_copy(row, sem, start=0, count=LAGS, left=0, width=cols):
         return pltpu.make_async_remote_copy(
@@ -193,6 +190,9 @@
     pl.when(has_up)(to_up.start)
     pl.when(has_down)(to_down.start)
 
+    for row in range(3, rows):
+        row_copy(row).start()
+    weight_copies[1].start()
     weight_copies[0].wait()
     space_row(1)
 
@@ -220,8 +220,7 @@
         time_part(row, [time_copy(row, row)])
 
     time_part(0, [time_copy(0, 0)])
-    for side in range(2):
-        time_part(last, [last_copies[side]], side * half, half)
+    time_part(last, last_copies)
 
     pl.when(has_up)(to_up.wait_send)
     pl.when(has_down)(to_down.wait_send)

time: 28.6 us -> 28.4 us (level)
  no operation moved by 1% of the time
where the time goes in v5:
time: 28.4 us; the launch traced here: 28.3 us
  Pallas kernels  27 us (95%)
  local copies, waits for them, and re-layouts  1.32 us (5%)
    pallas_call x1, Pallas kernels, body(): pl.pallas_call(kernel, out_shape=jax.ShapeDtypeStruct(features.shape, bf1...  27 us
    unnamed x1, local copies, waits for them, and re-layouts  1.32 us

profile of v5, /device:TPU:14, one launch (start us, length us, event | category | flops | bytes accessed | tf_op | source)
XLA Modules:
  0.0 28.3 jit_solution(7094834509739576972)
XLA Ops:
  0.0 27.0 %shard_map.73 = bf16[2,16,128,256]{3,2,1,0:T(8,128)(2,1)S(1)} custom-call(bf16[2,16,128,256]{3,2,1,0:T(8,128)(2,1)} %features.1, bf16[3,3,256,256]{3,2,1,0:T(8,128)(2,1)} %space_kernel.1, f32[256]{0:T(256)} %space_gain.1, f32[256]{0:T(256)} %space_bias.1, bf16[3,256,256]{2,1,0:T(8,128)(2,1)} %time_kernel.1, f32[256]{0:T(256)} %time_gain.1, f32[256]{0:T(256)} %time_bias.1), custom_call_target="tpu_custom_call" | custom-call | tf_op jit(solution)/shard_map/pallas_call | solution.py:241
  27.0 1.3 %copy.9 = bf16[2,16,128,256]{3,2,1,0:T(8,128)(2,1)} copy(bf16[2,16,128,256]{3,2,1,0:T(8,128)(2,1)S(1)} %shard_map.73) | data formatting | bytes 4194304

commit v6 on v5

--- a/solution.py
+++ b/solution.py
@@ -77,6 +77,9 @@
             device_id_type=pl.DeviceIdType.MESH,
         )
 
+    first_copies = [
+        time_copy(1, rows + 2 + start, start, 1) for start in range(LAGS)
+    ]
     last_copies = [
         time_copy(last, rows + side, 0, LAGS, side * half, half)
         for side in range(2)
@@ -194,7 +197,10 @@
         row_copy(row).start()
     weight_copies[1].start()
     weight_copies[0].wait()
-    space_row(1)
+    for start in reversed(range(frames)):
+        space_part(1, start, 1)
+        if start >= frames - LAGS:
+            pl.when(has_next)(first_copies[start - frames + LAGS].start)
 
     @pl.loop(2, last)
     def _(row):
@@ -215,7 +221,9 @@
             copy.start()
 
     weight_copies[1].wait()
-    @pl.loop(1, last)
+    time_part(1, first_copies)
+
+    @pl.loop(2, last)
     def _(row):
         time_part(row, [time_copy(row, row)])
 
@@ -227,10 +235,10 @@
 
     @pl.when(has_next)
     def _():
-        for copy in (time_copy(0, 0), *last_copies):
+        for copy in (time_copy(0, 0), *first_copies, *last_copies):
             copy.wait_send()
 
-        @pl.loop(1, last)
+        @pl.loop(2, last)
         def _(row):
             time_copy(row, row).wait_send()
 
@@ -256,8 +264,8 @@
             pltpu.SemaphoreType.DMA((6,)),
             pltpu.SemaphoreType.DMA((2,)),
             pltpu.SemaphoreType.DMA((2,)),
-            pltpu.SemaphoreType.DMA((rows + 2,)),
-            pltpu.SemaphoreType.DMA((rows + 2,)),
+            pltpu.SemaphoreType.DMA((rows + 2 + LAGS,)),
+            pltpu.SemaphoreType.DMA((rows + 2 + LAGS,)),
         ],
         compiler_params=pltpu.CompilerParams(
             collective_id=0, has_side_effects=True, vmem_limit_bytes=36 * 1024 * 1024

time: 28.4 us -> 28.4 us (level)
  no operation moved by 1% of the time
where the time goes in v6:
time: 28.4 us; the launch traced here: 28.3 us
  Pallas kernels  27 us (95%)
  local copies, waits for them, and re-layouts  1.32 us (5%)
    pallas_call x1, Pallas kernels, body(): pl.pallas_call(kernel, out_shape=jax.ShapeDtypeStruct(features.shape, bf1...  27 us
    unnamed x1, local copies, waits for them, and re-layouts  1.32 us

profile of v6, /device:TPU:14, one launch (start us, length us, event | category | flops | bytes accessed | tf_op | source)
XLA Modules:
  0.0 28.3 jit_solution(1272347098098672439)
XLA Ops:
  0.0 27.0 %shard_map.73 = bf16[2,16,128,256]{3,2,1,0:T(8,128)(2,1)S(1)} custom-call(bf16[2,16,128,256]{3,2,1,0:T(8,128)(2,1)} %features.1, bf16[3,3,256,256]{3,2,1,0:T(8,128)(2,1)} %space_kernel.1, f32[256]{0:T(256)} %space_gain.1, f32[256]{0:T(256)} %space_bias.1, bf16[3,256,256]{2,1,0:T(8,128)(2,1)} %time_kernel.1, f32[256]{0:T(256)} %time_gain.1, f32[256]{0:T(256)} %time_bias.1), custom_call_target="tpu_custom_call" | custom-call | tf_op jit(solution)/shard_map/pallas_call | solution.py:249
  27.0 1.3 %copy.9 = bf16[2,16,128,256]{3,2,1,0:T(8,128)(2,1)} copy(bf16[2,16,128,256]{3,2,1,0:T(8,128)(2,1)S(1)} %shard_map.73) | data formatting | bytes 4194304
